TPU v7x, 32 devices: a whole 2x2x4 slice. The times are simulated.
32 devices in a mesh: dp: 4 (over y, x), seq: 8 (over z, core).
Axes of the slice: x: 2, y: 2, z: 4, core: 2. Of those that a mesh axis runs over, the one named last changes fastest.
Arguments:
- tokens: bfloat16 [4, 1280, 2048], P('dp', 'seq'), may hold values from -6 to 6
- w_query: bfloat16 [2048, 2048], P(('dp', 'seq')), may hold values from -0.125 to 0.125
- w_key: bfloat16 [2048, 2048], P(('dp', 'seq')), may hold values from -0.125 to 0.125
- w_value: bfloat16 [2048, 2048], P(('dp', 'seq')), may hold values from -0.125 to 0.125
- w_out: bfloat16 [2048, 2048], P(None, ('dp', 'seq')), may hold values from -0.125 to 0.125
- w_gate: bfloat16 [2048, 8192], P(('dp', 'seq')), may hold values from -0.125 to 0.125
- w_up: bfloat16 [2048, 8192], P(('dp', 'seq')), may hold values from -0.125 to 0.125
- w_down: bfloat16 [8192, 2048], P(None, ('dp', 'seq')), may hold values from -0.0625 to 0.0625
- gain_query: bfloat16 [2048], P(('dp', 'seq')), may hold values from 0.5 to 1.5
- gain_key: bfloat16 [2048], P(('dp', 'seq')), may hold values from 0.5 to 1.5
- gain_attn: bfloat16 [2048], P(('dp', 'seq')), may hold values from 0.5 to 1.5
- gain_mlp: bfloat16 [2048], P(('dp', 'seq')), may hold values from 0.5 to 1.5
- cotangent: bfloat16 [4, 1280, 2048], P('dp', 'seq'), may hold values from -6 to 6
- key_mask: int32 [4, 1280], P('dp', 'seq'), may hold values 0 or 1
- lengths: int32 [4], P('dp'), may hold values from 640 to 1280, as said below
- tract_order: int32 [4, 16], P('dp', 'seq'), may hold values from 0 to 15, as said below
Outputs:
- layer_out: bfloat16 [4, 1280, 2048], P('dp', 'seq')
- grad_tokens: bfloat16 [4, 1280, 2048], P('dp', 'seq')
- grad_w_query: float32 [2048, 2048], P(('dp', 'seq'))
- grad_w_key: float32 [2048, 2048], P(('dp', 'seq'))
- grad_w_value: float32 [2048, 2048], P(('dp', 'seq'))
- grad_w_out: float32 [2048, 2048], P(None, ('dp', 'seq'))
- grad_w_gate: float32 [2048, 8192], P(('dp', 'seq'))
- grad_w_up: float32 [2048, 8192], P(('dp', 'seq'))
- grad_w_down: float32 [8192, 2048], P(None, ('dp', 'seq'))
- grad_gain_query: float32 [2048], P(('dp', 'seq'))
- grad_gain_key: float32 [2048], P(('dp', 'seq'))
- grad_gain_attn: float32 [2048], P(('dp', 'seq'))
- grad_gain_mlp: float32 [2048], P(('dp', 'seq'))
Inputs may be any that keep to these rules, and one draw needn't show every extreme that they name: `lengths`: some row has all 1280 tokens valid. `tract_order`: each row is a permutation of 0 to 15: entry j is the place, in units of 80 tokens, of the row's j-th stored block.
All inputs are finite; a program needn't handle non-finite values. No bound on the sum of `key_mask` on one device may be relied on, other than what follows from the above.
Results may differ from a plain program's by a relative error of at most 0.02.
Values may be sent and summed in bfloat16 or wider, within the bound.
A program may use at most 768 MiB of HBM per device.

v0:
```python
import jax
import jax.numpy as jnp
from jax import lax
from jax.sharding import PartitionSpec as P

HEAD_DIM = 128
rope_base = 500000.0
norm_eps = 1e-06
f32 = jnp.float32
bf16 = jnp.bfloat16


def rms_factor(values):
    return lax.rsqrt(jnp.mean(values * values, axis=-1, keepdims=True) + norm_eps)


def norm_back(grad_normed, raw_values, factor):
    unit_values = raw_values * factor
    return factor * (
        grad_normed - unit_values * jnp.mean(grad_normed * unit_values, axis=-1, keepdims=True)
    )


def rope_tables(positions, head_dim):
    half_dim = head_dim // 2
    steps_f = jnp.arange(half_dim).astype(f32) * (2.0 / head_dim)
    inv_freq = jnp.power(rope_base, -steps_f)
    angle = positions.astype(f32)[:, None] * inv_freq[None, :]
    angle = jnp.concatenate([angle, angle], axis=-1)[:, None, :]
    return (jnp.cos(angle), jnp.sin(angle))


def rotate(values, cosine, sine):
    half_dim = values.shape[-1] // 2
    turned = jnp.concatenate([-values[..., half_dim:], values[..., :half_dim]], axis=-1)
    return values * cosine + turned * sine


def unrotate(grads, cosine, sine):
    half_dim = grads.shape[-1] // 2
    moved = grads * sine
    back_part = jnp.concatenate([moved[..., half_dim:], -moved[..., :half_dim]], axis=-1)
    return grads * cosine + back_part


def allowed_mask(query_pos, key_code):
    key_pos = key_code // 2
    usable = key_code % 2 == 1
    causal = key_pos[None, :] <= query_pos[:, None]
    return causal & (usable[None, :] | (key_pos[None, :] == query_pos[:, None]))


def dot_nn(left, right):
    return jnp.dot(left, right, preferred_element_type=f32)


def dot_nt(left, right):
    return lax.dot_general(left, right, (((1,), (1,)), ((), ())), preferred_element_type=f32)


def dot_tn(left, right):
    return lax.dot_general(left, right, (((0,), (0,)), ((), ())), preferred_element_type=f32)


def spread_columns(parts, ways):
    rows = parts[0].shape[0]
    split = [p.reshape(rows, ways, p.shape[1] // ways) for p in parts]
    joined = jnp.concatenate(split, axis=2)
    return joined.reshape(rows, ways * joined.shape[2])


def collect(matrix):
    moved = lax.all_to_all(matrix, "seq", split_axis=1, concat_axis=0, tiled=True)
    return lax.all_gather(moved, "dp", axis=0, tiled=True)


def gather_rows(rows):
    return lax.all_gather(rows, "seq", axis=0, tiled=True)


def scatter_rows(partial_rows):
    return lax.psum_scatter(
        partial_rows.astype(bf16), "seq", scatter_dimension=0, tiled=True
    ).astype(f32)


def return_grads(grad, widths, ways):
    summed = lax.psum_scatter(grad.astype(bf16), "dp", scatter_dimension=0, tiled=True)
    rows = summed.shape[0] // ways
    moved = lax.all_to_all(summed, "seq", split_axis=0, concat_axis=1, tiled=True)
    moved = moved.reshape(rows, ways, sum(widths))
    outs, begin = ([], 0)
    for width in widths:
        outs.append(moved[:, :, begin : begin + width].reshape(rows, ways * width).astype(f32))
        begin += width
    return outs


def body(
    tokens,
    w_query,
    w_key,
    w_value,
    w_out,
    w_gate,
    w_up,
    w_down,
    gain_query,
    gain_key,
    gain_attn,
    gain_mlp,
    cotangent,
    key_mask,
    lengths,
    tract_order,
):
    ways = lax.axis_size("seq")
    me = lax.axis_index("seq")
    token_rows = tokens[0]
    tok_count, feat_width = token_rows.shape
    ff_width = w_gate.shape[1]
    own_feat = feat_width // ways
    own_heads = own_feat // HEAD_DIM
    own_ff = ff_width // ways
    row_len = tok_count * ways
    score_scale = HEAD_DIM ** (-0.5)
    half_len = tok_count // 2
    order_pair = tract_order[0]
    slot_index = jnp.arange(tok_count, dtype=jnp.int32)
    local_pos = (
        jnp.where(slot_index < half_len, order_pair[0], order_pair[1]) * half_len
        + slot_index % half_len
    )
    key_ok = ((key_mask[0] == 1) & (local_pos < lengths[0])).astype(jnp.int32)
    grad_out = cotangent[0].astype(f32)
    gain_local = jnp.stack([gain_query, gain_key, gain_attn, gain_mlp], axis=1)
    gain_pad = jnp.pad(gain_local, ((0, 0), (0, HEAD_DIM - 4)))
    gain_all = jnp.tile(gain_pad, (1, ways))
    m_qkv = collect(spread_columns([w_query, w_key, w_value], ways))
    m_out = collect(spread_columns([jnp.transpose(w_out), gain_all], ways))
    m_gu = collect(spread_columns([w_gate, w_up], ways))
    m_down = collect(spread_columns([jnp.transpose(w_down)], ways))
    gains = jnp.transpose(m_out[:, own_feat:])[:8].astype(f32)
    m_out = m_out[:, :own_feat]
    gain_q = lax.dynamic_slice_in_dim(gains[0], me * own_feat, own_feat, 0)
    gain_k = lax.dynamic_slice_in_dim(gains[1], me * own_feat, own_feat, 0)
    x_row = gather_rows(token_rows)
    key_code = gather_rows(local_pos * 2 + key_ok)
    pos = key_code // 2
    qkv = dot_nn(x_row, m_qkv)
    q_raw, k_raw, v_raw = (qkv[:, i * own_feat : (i + 1) * own_feat] for i in range(3))
    squares = lax.psum(
        jnp.stack([jnp.sum(q_raw * q_raw, axis=-1), jnp.sum(k_raw * k_raw, axis=-1)]), "seq"
    )
    factors = lax.rsqrt(squares / feat_width + norm_eps)
    q_factor, k_factor = (factors[0][:, None], factors[1][:, None])
    cosine, sine = rope_tables(pos, HEAD_DIM)
    head_shape = (row_len, own_heads, HEAD_DIM)
    query_low = rotate((q_raw * q_factor * gain_q).reshape(head_shape), cosine, sine).astype(bf16)
    key_low = rotate((k_raw * k_factor * gain_k).reshape(head_shape), cosine, sine).astype(bf16)
    value_low = v_raw.astype(bf16).reshape(head_shape)
    mask = allowed_mask(pos, key_code)[None]
    scores = (
        jnp.einsum("qhd,khd->hqk", query_low, key_low, preferred_element_type=f32) * score_scale
    )
    expo = jnp.where(mask, jnp.exp(scores), 0.0)
    weight_sum = jnp.transpose(jnp.sum(expo, axis=-1))[:, :, None]
    expo_low = expo.astype(bf16)
    attn = jnp.einsum("hqk,khd->qhd", expo_low, value_low, preferred_element_type=f32) / weight_sum
    attn_low = attn.astype(bf16).reshape(row_len, own_feat)
    branch = scatter_rows(dot_nt(attn_low, m_out))
    branch_factor = rms_factor(branch)
    branch_unit = branch * branch_factor
    hidden_in = token_rows.astype(f32) + branch_unit * gains[2]
    hidden_low = gather_rows(hidden_in.astype(bf16))
    gate_up = dot_nn(hidden_low, m_gu)
    gate_val, up_val = (gate_up[:, :own_ff], gate_up[:, own_ff:])
    sigma = jax.nn.sigmoid(gate_val)
    mixed_low = (gate_val * sigma * up_val).astype(bf16)
    mlp_val = scatter_rows(dot_nt(mixed_low, m_down))
    mlp_factor = rms_factor(mlp_val)
    mlp_unit = mlp_val * mlp_factor
    layer_out = hidden_in + mlp_unit * gains[3]
    grad_gain_mlp = jnp.sum(grad_out * mlp_unit, axis=0)
    grad_mlp = gather_rows(norm_back(grad_out * gains[3], mlp_val, mlp_factor).astype(bf16))
    grad_mixed = dot_nn(grad_mlp, m_down)
    grad_gate = grad_mixed * up_val * sigma * (1.0 + gate_val * (1.0 - sigma))
    grad_up = grad_mixed * gate_val * sigma
    grad_gu = jnp.concatenate([grad_gate, grad_up], axis=1).astype(bf16)
    grad_hidden = grad_out + scatter_rows(dot_nt(grad_gu, m_gu))
    dw_gu = return_grads(dot_tn(hidden_low, grad_gu), [own_ff, own_ff], ways)
    dw_down = return_grads(dot_tn(grad_mlp, mixed_low), [own_ff], ways)
    grad_gain_attn = jnp.sum(grad_hidden * branch_unit, axis=0)
    grad_branch = gather_rows(norm_back(grad_hidden * gains[2], branch, branch_factor).astype(bf16))
    grad_attn = dot_nn(grad_branch, m_out).reshape(head_shape)
    dw_out = return_grads(dot_tn(grad_branch, attn_low), [own_feat], ways)
    grad_num = (grad_attn / weight_sum).astype(bf16)
    drop = jnp.transpose(jnp.sum(grad_attn * attn, axis=-1) / weight_sum[:, :, 0])
    grad_expo = jnp.einsum("qhd,khd->hqk", grad_num, value_low, preferred_element_type=f32)
    grad_scores = (expo * (grad_expo - drop[:, :, None])).astype(bf16)
    grad_q = (
        jnp.einsum("hqk,khd->qhd", grad_scores, key_low, preferred_element_type=f32) * score_scale
    )
    grad_k = (
        jnp.einsum("hqk,qhd->khd", grad_scores, query_low, preferred_element_type=f32) * score_scale
    )
    grad_v = jnp.einsum("hqk,qhd->khd", expo_low, grad_num, preferred_element_type=f32)
    grad_q_norm = unrotate(grad_q, cosine, sine).reshape(row_len, own_feat)
    grad_k_norm = unrotate(grad_k, cosine, sine).reshape(row_len, own_feat)
    q_unit, k_unit = (q_raw * q_factor, k_raw * k_factor)
    grad_gain_query = jnp.sum(grad_q_norm * q_unit, axis=0)
    grad_gain_key = jnp.sum(grad_k_norm * k_unit, axis=0)
    c_q, c_k = (grad_q_norm * gain_q, grad_k_norm * gain_k)
    means = (
        lax.psum(jnp.stack([jnp.sum(c_q * q_unit, axis=-1), jnp.sum(c_k * k_unit, axis=-1)]), "seq")
        / feat_width
    )
    grad_q_raw = q_factor * (c_q - q_unit * means[0][:, None])
    grad_k_raw = k_factor * (c_k - k_unit * means[1][:, None])
    grad_qkv = jnp.concatenate(
        [grad_q_raw, grad_k_raw, grad_v.reshape(row_len, own_feat)], axis=1
    ).astype(bf16)
    grad_tokens = grad_hidden + scatter_rows(dot_nt(grad_qkv, m_qkv))
    own_slot = jnp.zeros((2, feat_width), f32)
    own_slot = lax.dynamic_update_slice(
        own_slot, jnp.stack([grad_gain_query, grad_gain_key]), (0, me * own_feat)
    )
    gain_terms = jnp.concatenate([own_slot, jnp.stack([grad_gain_attn, grad_gain_mlp])])
    gain_columns = jnp.pad(jnp.transpose(gain_terms), ((0, 0), (0, HEAD_DIM - 4)))
    dw_qkv = return_grads(
        jnp.concatenate([dot_tn(x_row, grad_qkv), gain_columns], axis=1),
        [own_feat] * 3 + [HEAD_DIM],
        ways,
    )
    gain_grads = jnp.sum(dw_qkv[3].reshape(-1, ways, HEAD_DIM), axis=1)
    gain_grads = jnp.transpose(gain_grads[:, :8])
    return (
        layer_out.astype(bf16)[None],
        grad_tokens.astype(bf16)[None],
        dw_qkv[0],
        dw_qkv[1],
        dw_qkv[2],
        jnp.transpose(dw_out[0]),
        dw_gu[0],
        dw_gu[1],
        jnp.transpose(dw_down[0]),
        gain_grads[0],
        gain_grads[1],
        gain_grads[2],
        gain_grads[3],
    )


def solution(mesh):
    both = ("dp", "seq")
    in_specs = (
        P("dp", "seq", None),
        P(both, None),
        P(both, None),
        P(both, None),
        P(None, both),
        P(both, None),
        P(both, None),
        P(None, both),
        P(both),
        P(both),
        P(both),
        P(both),
        P("dp", "seq", None),
        P("dp", "seq"),
        P("dp"),
        P("dp", "seq"),
    )
    out_specs = (
        P("dp", "seq", None),
        P("dp", "seq", None),
        P(both, None),
        P(both, None),
        P(both, None),
        P(None, both),
        P(both, None),
        P(both, None),
        P(None, both),
        P(both),
        P(both),
        P(both),
        P(both),
    )
    return jax.shard_map(body, mesh=mesh, in_specs=in_specs, out_specs=out_specs, check_vma=False)
```

profile of v0, /device:TPU:9, one launch (start us, length us, event | category | flops | bytes accessed | tf_op | source)
XLA Modules:
  0.0 1109.0 jit_solution(11077632735175738909)
XLA Ops:
  9.3 15.8 %all_to_all.125 = bf16[64,8,384]{2,0,1:T(8,128)(2,1)} all-to-all(bf16[64,8,384]{2,0,1:T(8,128)(2,1)S(1)} %copy.115), channel_id=1, replica_groups=mesh['dp'=4,'seq'=8] {'seq'}, dimensions={1} | all-to-all | bytes 786432 | tf_op jit(solution)/shard_map/all_to_all | solution.py:73
  25.6 23.3 %all_to_all.126 = bf16[64,8,768]{2,0,1:T(8,128)(2,1)} all-to-all(bf16[64,8,768]{2,0,1:T(8,128)(2,1)S(1)} %copy.113), channel_id=1, replica_groups=mesh['dp'=4,'seq'=8] {'seq'}, dimensions={1} | all-to-all | bytes 1572864 | tf_op jit(solution)/shard_map/all_to_all | solution.py:73
  53.6 6.9 all-reduce.2
  60.7 3.3 broadcast_multiply_fusion.3
  64.0 2.8 or_and_fusion
  69.7 32.8 %all-gather.10.cloned.1.call-done = bf16[2048,768]{1,0:T(8,128)(2,1)} async-done(((bf16[512,768]{1,0:T(8,128)(2,1)}), bf16[2048,768]{1,0:T(8,128)(2,1)}) %all-gather.10.cloned.1.call-update) | async-done | bytes 3145744 | tf_op jit(solution)/shard_map/all_gather | solution.py:74
  102.5 56.4 %all-gather.24.cloned.1.call-done = bf16[1,1280,2048]{2,1,0:T(8,128)(2,1)} async-done(((bf16[1,160,2048]{2,1,0:T(8,128)(2,1)}), bf16[1,1280,2048]{2,1,0:T(8,128)(2,1)}) %all-gather.24.cloned.1.call-update) | async-done | bytes 5242896 | tf_op jit(solution)/shard_map/all_gather | solution.py:78
  158.9 7.7 fusion.7
  168.6 22.2 %psum.14 = f32[2,1280]{1,0:T(2,128)S(1)} all-reduce(f32[2,1280]{1,0:T(2,128)S(1)} %pad_maximum_fusion.10), channel_id=1, replica_groups=mesh['dp'=4,'seq'=8] {'seq'}, use_global_device_ids=true, to_apply=%region_2.3 | all-reduce | flops 2560 | bytes 20480 | tf_op jit(solution)/shard_map/psum | solution.py:152
  194.5 3.5 fusion.83
  200.3 3.1 copy-done
  204.2 3.8 convolution_convert_fusion.4
  211.9 88.8 %all_to_all.127 = bf16[64,8,2048]{2,0,1:T(8,128)(2,1)} all-to-all(bf16[64,8,2048]{2,0,1:T(8,128)(2,1)S(1)} %copy.119), channel_id=1, replica_groups=mesh['dp'=4,'seq'=8] {'seq'}, dimensions={1} | all-to-all | bytes 4194304 | tf_op jit(solution)/shard_map/all_to_all | solution.py:73
  300.8 15.4 %reduce-scatter.9.cloned.1.call-done = bf16[160,2048]{1,0:T(8,128)(2,1)} async-done(((bf16[1280,2048]{1,0:T(8,128)(2,1)}), bf16[160,2048]{1,0:T(8,128)(2,1)}) %reduce-scatter.9.cloned.1.call-update) | async-done | bytes 655376 | tf_op jit(solution)/shard_map/reduce_scatter | solution.py:82
  319.9 27.2 %all_to_all.128 = bf16[64,8,1024]{2,0,1:T(8,128)(2,1)} all-to-all(bf16[64,8,1024]{2,0,1:T(8,128)(2,1)S(1)} %bitcast.187), channel_id=1, replica_groups=mesh['dp'=4,'seq'=8] {'seq'}, dimensions={1} | all-to-all | bytes 2097152 | tf_op jit(solution)/shard_map/all_to_all | solution.py:73
  347.6 57.2 %all-gather.16.cloned.1.call-done = bf16[2048,2048]{1,0:T(8,128)(2,1)} async-done(((bf16[512,2048]{1,0:T(8,128)(2,1)}), bf16[2048,2048]{1,0:T(8,128)(2,1)}) %all-gather.16.cloned.1.call-update) | async-done | bytes 8388624 | tf_op jit(solution)/shard_map/all_gather | solution.py:74
  404.9 56.8 %all-gather.14.cloned.1.call-done = bf16[1280,2048]{1,0:T(8,128)(2,1)} async-done(((bf16[160,2048]{1,0:T(8,128)(2,1)}), bf16[1280,2048]{1,0:T(8,128)(2,1)}) %all-gather.14.cloned.1.call-update) | async-done | bytes 5242896 | tf_op jit(solution)/shard_map/all_gather | solution.py:78
  461.7 15.2 %fusion.85 = f32[1280,2048]{1,0:T(8,128)S(1)} fusion(bf16[1280,2048]{1,0:T(8,128)(2,1)} %all-gather.14.cloned.1.call-done, bf16[2048,2048]{1,0:T(8,128)(2,1)} %all-gather.16.cloned.1.call-done), kind=kOutput, calls=%fused_computation.180 | convolution fusion | flops 10737418240 | bytes 24117248 | tf_op jit(solution)/shard_map/dot_general | solution.py:54
  476.9 3.9 copy-done.5
  480.8 2.7 multiply_convert_fusion.2
  483.5 32.9 %all-gather.18.cloned.1.call-done = bf16[2048,1024]{1,0:T(8,128)(2,1)} async-done(((bf16[512,1024]{1,0:T(8,128)(2,1)}), bf16[2048,1024]{1,0:T(8,128)(2,1)}) %all-gather.18.cloned.1.call-update) | async-done | bytes 4194320 | tf_op jit(solution)/shard_map/all_gather | solution.py:74
  516.4 9.9 convolution_convert_fusion.3
  526.4 58.5 %reduce-scatter.11.cloned.1.call-done = bf16[160,2048]{1,0:T(8,128)(2,1)} async-done(((bf16[1280,2048]{1,0:T(8,128)(2,1)}), bf16[160,2048]{1,0:T(8,128)(2,1)}) %reduce-scatter.11.cloned.1.call-update) | async-done | bytes 655376 | tf_op jit(solution)/shard_map/reduce_scatter | solution.py:82
  589.4 54.5 %all-gather.20.cloned.1.call-done = bf16[1280,2048]{1,0:T(8,128)(2,1)} async-done(((bf16[160,2048]{1,0:T(8,128)(2,1)}), bf16[1280,2048]{1,0:T(8,128)(2,1)}) %all-gather.20.cloned.1.call-update) | async-done | bytes 5242896 | tf_op jit(solution)/shard_map/all_gather | solution.py:78
  643.9 13.1 %multiply_convert_fusion.1 = (bf16[1280,1024]{1,0:T(8,128)(2,1)S(1)}, bf16[1280,1024]{1,0:T(8,128)(2,1)S(1)}) fusion(f32[1280,2048]{1,0:T(8,128)} %copy-done.5, bf16[1280,2048]{1,0:T(8,128)(2,1)} %all-gather.20.cloned.1.call-done, bf16[2048,1024]{1,0:T(8,128)(2,1)} %all-gather.18.cloned.1.call-done), kind=kOutput, calls=%fused_computation.19 | convolution fusion | flops 5385748480 | bytes 25165824 | tf_op jit(solution)/shard_map/dot_general | solution.py:54
  659.3 15.3 %convolution_convert_fusion.2 = bf16[1280,2048]{1,0:T(8,128)(2,1)} fusion(bf16[2048,2048]{1,0:T(8,128)(2,1)} %all-gather.16.cloned.1.call-done, bf16[1280,1024]{1,0:T(8,128)(2,1)S(1)} %get-tuple-element.38, bf16[1280,1024]{1,0:T(8,128)(2,1)S(1)} %get-tuple-element.37), kind=kOutput, calls=%fused_computation.7 | convolution fusion | flops 10750525440 | bytes 18874368 | tf_op jit(solution)/shard_map/dot_general | solution.py:58
  674.7 58.6 %reduce-scatter.13.cloned.1.call-done = bf16[160,2048]{1,0:T(8,128)(2,1)} async-done(((bf16[1280,2048]{1,0:T(8,128)(2,1)}), bf16[160,2048]{1,0:T(8,128)(2,1)}) %reduce-scatter.13.cloned.1.call-update) | async-done | bytes 655376 | tf_op jit(solution)/shard_map/reduce_scatter | solution.py:82
  737.1 10.2 convolution_convert_fusion.5
  747.6 16.7 %convolution_convert_fusion = bf16[2048,2048]{1,0:T(8,128)(2,1)} fusion(bf16[1280,2048]{1,0:T(8,128)(2,1)} %all-gather.14.cloned.1.call-done, bf16[1280,1024]{1,0:T(8,128)(2,1)} %copy-done.42, bf16[1280,1024]{1,0:T(8,128)(2,1)} %copy-done.41), kind=kOutput, calls=%fused_computation.5 | convolution fusion | flops 10752098304 | bytes 18874368 | tf_op jit(solution)/shard_map/dot_general | solution.py:62
  764.4 27.4 %all-gather.22.cloned.1.call-done = bf16[1280,2048]{1,0:T(8,128)(2,1)} async-done(((bf16[160,2048]{1,0:T(8,128)(2,1)}), bf16[1280,2048]{1,0:T(8,128)(2,1)}) %all-gather.22.cloned.1.call-update) | async-done | bytes 5242896 | tf_op jit(solution)/shard_map/all_gather | solution.py:78
  791.8 4.7 multiply_reduce_fusion.2
  796.6 6.3 fusion.1
  810.4 23.1 %psum.15 = f32[2,1280]{1,0:T(2,128)S(1)} all-reduce(f32[2,1280]{1,0:T(2,128)S(1)} %pad_maximum_fusion.11), channel_id=1, replica_groups=mesh['dp'=4,'seq'=8] {'seq'}, use_global_device_ids=true, to_apply=%region_14.15 | all-reduce | flops 2560 | bytes 20480 | tf_op jit(solution)/shard_map/psum | solution.py:215
  833.6 5.3 convolution_convert_fusion.6
  839.0 2.6 multiply_convert_fusion.4
  841.7 7.5 fusion.27
  849.2 5.6 fusion.18
  854.8 2.3 fusion.10
  858.7 8.0 convolution_convert_fusion.1
  866.7 33.6 %all_to_all.129 = bf16[8,64,1024]{2,1,0:T(8,128)(2,1)} all-to-all(bf16[8,64,1024]{2,1,0:T(8,128)(2,1)} %bitcast.201), channel_id=1, replica_groups=mesh['dp'=4,'seq'=8] {'seq'}, dimensions={0} | all-to-all | bytes 2097152 | tf_op jit(solution)/shard_map/all_to_all | solution.py:90
  900.3 36.9 %reduce-scatter.21.cloned.1.call-done = bf16[512,2048]{1,0:T(8,128)(2,1)} async-done(((bf16[2048,2048]{1,0:T(8,128)(2,1)}), bf16[512,2048]{1,0:T(8,128)(2,1)}) %reduce-scatter.21.cloned.1.call-update) | async-done | bytes 2097168 | tf_op jit(solution)/shard_map/reduce_scatter | solution.py:88
  937.2 51.5 %all_to_all.130 = bf16[8,64,2048]{2,1,0:T(8,128)(2,1)S(1)} all-to-all(bf16[8,64,2048]{2,1,0:T(8,128)(2,1)} %bitcast.192), channel_id=1, replica_groups=mesh['dp'=4,'seq'=8] {'seq'}, dimensions={0} | all-to-all | bytes 4194304 | tf_op jit(solution)/shard_map/all_to_all | solution.py:90
  988.7 6.3 all-to-all-start.5
  995.1 24.7 %reduce-scatter.17.cloned.1.call-done = bf16[512,896]{0,1:T(8,128)(2,1)} async-done(((bf16[2048,896]{0,1:T(8,128)(2,1)}), bf16[512,896]{0,1:T(8,128)(2,1)}) %reduce-scatter.17.cloned.1.call-update) | async-done | bytes 917520 | tf_op jit(solution)/shard_map/reduce_scatter | solution.py:88
  1022.0 5.5 all-to-all-start.4
  1034.7 26.6 %all-to-all-done.4 = bf16[8,64,896]{2,1,0:T(8,128)(2,1)} async-done(((bf16[8,64,896]{2,1,0:T(8,128)(2,1)}), bf16[8,64,896]{2,1,0:T(8,128)(2,1)}, u32[]{:S(2)}, u32[]{:S(2)}) %all-to-all-start.4) | async-done | bytes 917536 | tf_op jit(solution)/shard_map/all_to_all | solution.py:90
  1066.8 33.0 %reduce-scatter.15.cloned.1.call-done = bf16[160,2048]{1,0:T(8,128)(2,1)} async-done(((bf16[1280,2048]{1,0:T(8,128)(2,1)}), bf16[160,2048]{1,0:T(8,128)(2,1)}) %reduce-scatter.15.cloned.1.call-update) | async-done | bytes 655376 | tf_op jit(solution)/shard_map/reduce_scatter | solution.py:82
  1099.8 2.2 fusion.64
  (210 shorter events, 60.7 us)
Async XLA Ops:
  7.2 18.0 %copy-start.27 = (bf16[64,2048]{1,0:T(8,128)(2,1)S(1)}, bf16[64,2048]{1,0:T(8,128)(2,1)}, u32[]{:S(2)}) copy-start(bf16[64,2048]{1,0:T(8,128)(2,1)} %param.17) | copy-start | bytes 786436
  7.2 18.1 %copy-start.28 = (bf16[64,2048]{1,0:T(8,128)(2,1)S(1)}, bf16[64,2048]{1,0:T(8,128)(2,1)}, u32[]{:S(2)}) copy-start(bf16[64,2048]{1,0:T(8,128)(2,1)} %param.18) | copy-start | bytes 786436
  7.2 59.6 %all-gather.12.cloned.1.call-start = ((), (), s32[]{:S(2)}) async-start(), calls=%async_computation.17 | async-start | bytes 1966080 | tf_op jit(solution)/shard_map/all_gather | solution.py:74
  8.3 17.0 %copy-start.29 = (bf16[64,2048]{1,0:T(8,128)(2,1)S(1)}, bf16[64,2048]{1,0:T(8,128)(2,1)}, u32[]{:S(2)}) copy-start(bf16[64,2048]{1,0:T(8,128)(2,1)} %param.19) | copy-start | bytes 786436
  25.1 77.4 %all-gather.10.cloned.1.call-start = ((), (), s32[]{:S(2)}) async-start(), calls=%async_computation.16 | async-start | bytes 3932160 | tf_op jit(solution)/shard_map/all_gather | solution.py:74
  25.4 24.9 %copy-start.40 = (u32[32]{0:T(128)S(1)}, u32[32]{0:T(128)}, u32[]{:S(2)}) copy-start(u32[32]{0:T(128)} %constant.93) | copy-start | bytes 388
  25.5 26.1 %copy-start.38 = (s32[1,2]{1,0:T(1,128)S(1)}, s32[1,2]{1,0:T(1,128)}, u32[]{:S(2)}) copy-start(s32[1,2]{1,0:T(1,128)} %param.31) | copy-start | bytes 28
  25.5 26.7 %copy-start.39 = (s32[1,160]{1,0:T(1,128)S(1)}, s32[1,160]{1,0:T(1,128)}, u32[]{:S(2)}) copy-start(s32[1,160]{1,0:T(1,128)} %param.29) | copy-start | bytes 1924
  48.9 109.9 %all-gather.24.cloned.1.call-start = ((), (), s32[]{:S(2)}) async-start(), calls=%async_computation.31 | async-start | bytes 5898240 | tf_op jit(solution)/shard_map/all_gather | solution.py:78
  49.7 266.6 %reduce-scatter.9.cloned.1.call-start = ((), (), s32[]{:S(2)}) async-start(), calls=%async_computation.18 | async-start | bytes 5898240 | tf_op jit(solution)/shard_map/reduce_scatter | solution.py:82
  69.6 121.2 %copy-start.34 = (f32[256]{0:T(256)}, f32[256]{0:T(256)S(1)}, u32[]{:S(2)}) copy-start(f32[256]{0:T(256)S(1)} %get-tuple-element.79) | copy-start | bytes 3076
  69.6 121.2 %copy-start.36 = (f32[256]{0:T(256)}, f32[256]{0:T(256)S(1)}, u32[]{:S(2)}) copy-start(f32[256]{0:T(256)S(1)} %get-tuple-element.80) | copy-start | bytes 3076
  193.7 4.4 copy-start.16
  198.1 5.3 copy-start
  198.1 6.1 copy-start.19
  208.1 196.8 %all-gather.16.cloned.1.call-start = ((), (), s32[]{:S(2)}) async-start(), calls=%async_computation.20 | async-start | bytes 10485760 | tf_op jit(solution)/shard_map/all_gather | solution.py:74
  300.7 16.8 %copy-start.10 = (bf16[1,160,2048]{2,1,0:T(8,128)(2,1)S(1)}, bf16[1,160,2048]{2,1,0:T(8,128)(2,1)}, u32[]{:S(2)}) copy-start(bf16[1,160,2048]{2,1,0:T(8,128)(2,1)} %param.16) | copy-start | bytes 1966084
  300.7 19.1 %copy-start.22 = (bf16[8192,64]{0,1:T(8,128)(2,1)S(1)}, bf16[8192,64]{0,1:T(8,128)(2,1)}, u32[]{:S(2)}) copy-start(bf16[8192,64]{0,1:T(8,128)(2,1)} %param.23) | copy-start | bytes 3145732
  300.7 160.9 %all-gather.14.cloned.1.call-start = ((), (), s32[]{:S(2)}) async-start(), calls=%async_computation.19 | async-start | bytes 5898240 | tf_op jit(solution)/shard_map/all_gather | solution.py:78
  319.8 196.6 %all-gather.18.cloned.1.call-start = ((), (), s32[]{:S(2)}) async-start(), calls=%async_computation.21 | async-start | bytes 5242880 | tf_op jit(solution)/shard_map/all_gather | solution.py:74
  347.2 237.7 %reduce-scatter.11.cloned.1.call-start = ((), (), s32[]{:S(2)}) async-start(), calls=%async_computation.22 | async-start | bytes 5898240 | tf_op jit(solution)/shard_map/reduce_scatter | solution.py:82
  476.9 3.9 copy-start.5
  526.3 60.0 %copy-start.3 = (bf16[1,160,2048]{2,1,0:T(8,128)(2,1)S(1)}, bf16[1,160,2048]{2,1,0:T(8,128)(2,1)}, u32[]{:S(2)}) copy-start(bf16[1,160,2048]{2,1,0:T(8,128)(2,1)} %param.28) | copy-start | bytes 1966084
  526.3 117.6 %all-gather.20.cloned.1.call-start = ((), (), s32[]{:S(2)}) async-start(), calls=%async_computation.23 | async-start | bytes 5898240 | tf_op jit(solution)/shard_map/all_gather | solution.py:78
  584.9 3.1 copy-start.6
  589.2 144.2 %reduce-scatter.13.cloned.1.call-start = ((), (), s32[]{:S(2)}) async-start(), calls=%async_computation.24 | async-start | bytes 5898240 | tf_op jit(solution)/shard_map/reduce_scatter | solution.py:82
  657.1 2.3 copy-start.42
  674.6 58.7 %copy-start.4 = (bf16[160,2048]{1,0:T(8,128)(2,1)S(1)}, bf16[160,2048]{1,0:T(8,128)(2,1)}, u32[]{:S(2)}) copy-start(bf16[160,2048]{1,0:T(8,128)(2,1)} %reduce-scatter.9.cloned.1.call-done) | copy-start | bytes 1966084
  674.7 117.1 %all-gather.22.cloned.1.call-start = ((), (), s32[]{:S(2)}) async-start(), calls=%async_computation.25 | async-start | bytes 5898240 | tf_op jit(solution)/shard_map/all_gather | solution.py:78
  737.1 129.6 %reduce-scatter.23.cloned.1.call-start = ((), (), s32[]{:S(2)}) async-start(), calls=%async_computation.30 | async-start | bytes 5242880 | tf_op jit(solution)/shard_map/reduce_scatter | solution.py:88
  747.3 189.9 %reduce-scatter.21.cloned.1.call-start = ((), (), s32[]{:S(2)}) async-start(), calls=%async_computation.29 | async-start | bytes 10485760 | tf_op jit(solution)/shard_map/reduce_scatter | solution.py:88
  764.3 224.5 %reduce-scatter.19.cloned.1.call-start = ((), (), s32[]{:S(2)}) async-start(), calls=%async_computation.28 | async-start | bytes 1310720 | tf_op jit(solution)/shard_map/reduce_scatter | solution.py:88
  796.5 6.4 copy-start.12
  796.5 6.3 copy-start.17
  802.9 2.2 copy-start.7
  807.5 2.1 copy-start.31
  807.5 2.2 copy-start.33
  807.5 2.2 copy-start.35
  838.9 180.8 %reduce-scatter.17.cloned.1.call-start = ((), (), s32[]{:S(2)}) async-start(), calls=%async_computation.27 | async-start | bytes 4587520 | tf_op jit(solution)/shard_map/reduce_scatter | solution.py:88
  839.0 2.7 copy-start.13
  839.0 10.2 slice-start
  841.6 7.6 copy-start.23
  841.6 7.6 copy-start.25
  841.7 7.5 slice-start.1
  857.1 242.6 %reduce-scatter.15.cloned.1.call-start = ((), (), s32[]{:S(2)}) async-start(), calls=%async_computation.26 | async-start | bytes 5898240 | tf_op jit(solution)/shard_map/reduce_scatter | solution.py:82
  988.7 33.2 %all-to-all-start.5 = ((bf16[8,64,256]{2,1,0:T(8,128)(2,1)}), bf16[8,64,256]{2,1,0:T(8,128)(2,1)S(1)}, u32[]{:S(2)}, u32[]{:S(2)}) async-start(bf16[8,64,256]{2,1,0:T(8,128)(2,1)} %bitcast.218), calls=%async_computation.11 | async-start | bytes 524288 | tf_op jit(solution)/shard_map/all_to_all | solution.py:90
  1022.0 39.3 %all-to-all-start.4 = ((bf16[8,64,896]{2,1,0:T(8,128)(2,1)}), bf16[8,64,896]{2,1,0:T(8,128)(2,1)}, u32[]{:S(2)}, u32[]{:S(2)}) async-start(bf16[8,64,896]{2,1,0:T(8,128)(2,1)} %bitcast.190), calls=%async_computation.9 | async-start | bytes 1835008 | tf_op jit(solution)/shard_map/all_to_all | solution.py:90
  1062.5 37.2 %copy-start.9 = (bf16[160,2048]{1,0:T(8,128)(2,1)S(1)}, bf16[160,2048]{1,0:T(8,128)(2,1)}, u32[]{:S(2)}) copy-start(bf16[160,2048]{1,0:T(8,128)(2,1)} %reduce-scatter.13.cloned.1.call-done) | copy-start | bytes 1966084
  (15 other events, 24.7 us)
Sparse Core Ops, SparseCore 0:
  25.2 31.3 all-gather.11
  58.5 43.9 all-gather.9
  104.1 54.6 all-gather.23
  208.2 107.9 reduce-scatter.8
  317.9 86.8 all-gather.15
  406.9 54.6 all-gather.13
  463.5 52.8 all-gather.17
  526.4 58.3 reduce-scatter.10
  589.3 54.5 all-gather.19
  674.8 58.5 reduce-scatter.12
  737.2 54.5 all-gather.21
  794.6 52.8 reduce-scatter.22
  850.8 86.3 reduce-scatter.20
  940.5 27.7 reduce-scatter.18
  971.4 48.3 reduce-scatter.16
  1022.0 77.6 reduce-scatter.14
where the time goes:
time: 1120 us; the launch traced here: 1110 us
  waiting for transfers between devices  573 us (51%)
  blocking collectives  292 us (26%)
  matrix products  138 us (12%)
  other arithmetic  38.8 us (3%)
  local copies, waits for them, and re-layouts  36.8 us (3%)
  between operations  16.6 us (1%)
  starting transfers between devices  13.3 us (1%)
    all_gather x4, waiting for transfers between devices, gather_rows(): return lax.all_gather(rows, 'seq', axis=0, tiled=True)  195 us
    reduce_scatter x4, waiting for transfers between devices, scatter_rows(): lax.psum_scatter(partial_rows.astype(bf16), 'seq', scatter_dimension=0, t...  166 us
    all_to_all x4, blocking collectives, collect(): lax.all_to_all(matrix, 'seq', split_axis=1, concat_axis=0, tiled=True)  155 us
    all_gather x4, waiting for transfers between devices, collect(): return lax.all_gather(moved, 'dp', axis=0, tiled=True)  123 us
    all_to_all x2, blocking collectives, return_grads(): lax.all_to_all(summed, 'seq', split_axis=0, concat_axis=1, tiled=True)  85.1 us
    reduce_scatter x4, waiting for transfers between devices, return_grads(): lax.psum_scatter(grad.astype(bf16), 'dp', scatter_dimension=0, tiled=True)  61.6 us
    dot_general x4, matrix products, dot_nn(): return jnp.dot(left, right, preferred_element_type=f32)  40.8 us
    dot_general x4, matrix products, dot_tn(): lax.dot_general(left, right, (((0,), (0,)), ((), ())), preferred_element_...  37.7 us
  transfers between devices with their start and end apart: 18, of which 14 were waited for; matrix products, arithmetic and copies ran while one was open for 11% of the time, Pallas kernels for 0%

commit v1 on v0

--- a/solution.py
+++ b/solution.py
@@ -8,6 +8,18 @@
 norm_eps = 1e-06
 f32 = jnp.float32
 bf16 = jnp.bfloat16
+
+
+def collect_2(x, axis, dim):
+    ways, here, hop = (lax.axis_size(axis), lax.axis_index(axis), x.shape[dim])
+    line, have = (x, 1)
+    while have < ways:
+        line = jnp.concatenate(
+            [line, lax.ppermute(line, axis, [(d, (d - have) % ways) for d in range(ways)])],
+            axis=dim,
+        )
+        have = 2 * have
+    return jnp.roll(line, here * hop, axis=dim)
 
 
 def rms_factor(values):
@@ -71,7 +83,7 @@
 
 def collect(matrix):
     moved = lax.all_to_all(matrix, "seq", split_axis=1, concat_axis=0, tiled=True)
-    return lax.all_gather(moved, "dp", axis=0, tiled=True)
+    return collect_2(moved, "dp", 0)
 
 
 def gather_rows(rows):

time: 1120 us -> 1170 us (1.045)
  blocking collectives: 292 us -> 198 us
  waiting for transfers between devices: 573 us -> 650 us
  starting transfers between devices: 13.3 us -> 56.8 us
  local copies, waits for them, and re-layouts: 36.8 us -> 61.5 us
    ppermute x0 -> x8, waiting for transfers between devices: none -> 171 us  [collect_2(): lax.ppermute(line, axis, [(d, (d - have) % ways) for d in range(ways)])]
    all_gather x4 -> x0, waiting for transfers between devices: 123 us -> none  [collect(): return lax.all_gather(moved, 'dp', axis=0, tiled=True)]
    all_gather x4, waiting for transfers between devices: 195 us -> 81.6 us  [gather_rows(): return lax.all_gather(rows, 'seq', axis=0, tiled=True)]
    reduce_scatter x4, waiting for transfers between devices: 166 us -> 275 us  [scatter_rows(): lax.psum_scatter(partial_rows.astype(bf16), 'seq', scatter_dimension=0, t...]
    all_to_all x4 -> x1, blocking collectives: 155 us -> 53.2 us  [collect(): lax.all_to_all(matrix, 'seq', split_axis=1, concat_axis=0, tiled=True)]
    all_to_all x0 -> x3, waiting for transfers between devices: none -> 33 us  [collect(): lax.all_to_all(matrix, 'seq', split_axis=1, concat_axis=0, tiled=True)]
    all_to_all x0 -> x3, starting transfers between devices: none -> 22.1 us  [collect(): lax.all_to_all(matrix, 'seq', split_axis=1, concat_axis=0, tiled=True)]
    ppermute x0 -> x8, starting transfers between devices: none -> 21.6 us  [collect_2(): lax.ppermute(line, axis, [(d, (d - have) % ways) for d in range(ways)])]
  transfers between devices with their start and end apart: 18 -> 25, of which waited for: 14 -> 15; matrix products, arithmetic and copies ran while one was open for 11% -> 11% of each run, Pallas kernels for 0% -> 0%
where the time goes in v1:
time: 1170 us; the launch traced here: 1160 us
  waiting for transfers between devices  650 us (56%)
  blocking collectives  198 us (17%)
  matrix products  140 us (12%)
  local copies, waits for them, and re-layouts  61.5 us (5%)
  starting transfers between devices  56.8 us (5%)
  other arithmetic  41 us (4%)
  between operations  17 us (1%)
    reduce_scatter x4, waiting for transfers between devices, scatter_rows(): lax.psum_scatter(partial_rows.astype(bf16), 'seq', scatter_dimension=0, t...  275 us
    ppermute x8, waiting for transfers between devices, collect_2(): lax.ppermute(line, axis, [(d, (d - have) % ways) for d in range(ways)])  171 us
    all_to_all x2, blocking collectives, return_grads(): lax.all_to_all(summed, 'seq', split_axis=0, concat_axis=1, tiled=True)  85 us
    all_gather x4, waiting for transfers between devices, gather_rows(): return lax.all_gather(rows, 'seq', axis=0, tiled=True)  81.6 us
    reduce_scatter x4, waiting for transfers between devices, return_grads(): lax.psum_scatter(grad.astype(bf16), 'dp', scatter_dimension=0, tiled=True)  61.7 us
    all_to_all x1, blocking collectives, collect(): lax.all_to_all(matrix, 'seq', split_axis=1, concat_axis=0, tiled=True)  53.2 us
    dot_general x4, matrix products, dot_nn(): return jnp.dot(left, right, preferred_element_type=f32)  40.5 us
    unnamed x119, local copies, waits for them, and re-layouts  39 us
  transfers between devices with their start and end apart: 25, of which 15 were waited for; matrix products, arithmetic and copies ran while one was open for 11% of the time, Pallas kernels for 0%

profile of v1, /device:TPU:9, one launch (start us, length us, event | category | flops | bytes accessed | tf_op | source)
XLA Modules:
  0.0 1164.6 jit_solution(1013503327694734546)
XLA Ops:
  10.7 5.6 all-to-all-start.1
  21.6 12.5 %all-reduce.2 = s32[1280]{0:T(1024)S(1)} all-reduce(s32[1280]{0:T(1024)S(1)} %fusion.90), channel_id=1, replica_groups=mesh['dp'=4,'seq'=8] {'seq'}, use_global_device_ids=true, to_apply=%add.2 | all-reduce | flops 1280 | bytes 10240
  34.1 6.8 all-to-all-start
  40.9 2.8 or_and_fusion
  46.0 33.0 %all-to-all-done = bf16[64,8,768]{2,0,1:T(8,128)(2,1)S(1)} async-done(((bf16[64,8,768]{2,0,1:T(8,128)(2,1)}), bf16[64,8,768]{2,0,1:T(8,128)(2,1)S(1)}, u32[]{:S(2)}, u32[]{:S(2)}) %all-to-all-start) | async-done | bytes 786464 | tf_op jit(solution)/shard_map/all_to_all | solution.py:85
  81.5 3.5 broadcast_multiply_fusion.3
  86.1 11.6 collective-permute-done
  104.5 28.6 %collective-permute-done.1 = bf16[1024,768]{1,0:T(8,128)(2,1)S(1)} collective-permute-done((bf16[1024,768]{1,0:T(8,128)(2,1)S(1)}, bf16[1024,768]{1,0:T(8,128)(2,1)S(1)}, u32[]{:S(2)}, u32[]{:S(2)}) %collective-permute-start.1) | collective-permute-done | bytes 1572896 | tf_op jit(solution)/shard_map/ppermute | solution.py:18
  137.5 7.7 fusion.10
  147.2 25.0 %psum.14 = f32[2,1280]{1,0:T(2,128)S(1)} all-reduce(f32[2,1280]{1,0:T(2,128)S(1)} %pad_maximum_fusion.14), channel_id=1, replica_groups=mesh['dp'=4,'seq'=8] {'seq'}, use_global_device_ids=true, to_apply=%region_2.3 | all-reduce | flops 2560 | bytes 20480 | tf_op jit(solution)/shard_map/psum | solution.py:164
  177.1 3.5 fusion.99
  180.6 2.7 fusion.100
  186.5 5.1 convolution_convert_fusion.4
  196.8 9.7 all-to-all-start.2
  206.4 97.6 %reduce-scatter.9.cloned.1.call-done = bf16[160,2048]{1,0:T(8,128)(2,1)} async-done(((bf16[1280,2048]{1,0:T(8,128)(2,1)}), bf16[160,2048]{1,0:T(8,128)(2,1)}) %reduce-scatter.9.cloned.1.call-update) | async-done | bytes 655376 | tf_op jit(solution)/shard_map/reduce_scatter | solution.py:94
  307.9 12.4 %collective-permute-start.4 = (bf16[512,2048]{1,0:T(8,128)(2,1)S(1)}, bf16[512,2048]{1,0:T(8,128)(2,1)S(1)}, u32[]{:S(2)}, u32[]{:S(2)}) collective-permute-start(bf16[512,2048]{1,0:T(8,128)(2,1)S(1)} %bitcast.168), channel_id=1, source_target_pairs={{0,24},{8,0},{16,8},{24,16},{1,25},{9,1},{17,9},{25,17},{2,26},{10... | collective-permute-start | bytes 6291464 | tf_op jit(solution)/shard_map/ppermute | solution.py:18
  321.6 53.2 %all_to_all.125 = bf16[64,8,1024]{2,0,1:T(8,128)(2,1)S(1)} all-to-all(bf16[64,8,1024]{2,0,1:T(8,128)(2,1)S(1)} %bitcast.193), channel_id=1, replica_groups=mesh['dp'=4,'seq'=8] {'seq'}, dimensions={1} | all-to-all | bytes 2097152 | tf_op jit(solution)/shard_map/all_to_all | solution.py:85
  376.0 21.2 %collective-permute-done.6 = bf16[512,1024]{1,0:T(8,128)(2,1)S(1)} collective-permute-done((bf16[512,1024]{1,0:T(8,128)(2,1)S(1)}, bf16[512,1024]{1,0:T(8,128)(2,1)S(1)}, u32[]{:S(2)}, u32[]{:S(2)}) %collective-permute-start.6) | collective-permute-done | bytes 1048608 | tf_op jit(solution)/shard_map/ppermute | solution.py:18
  397.4 2.6 collective-permute-start.7
  401.6 108.6 %collective-permute-done.7 = bf16[1024,1024]{1,0:T(8,128)(2,1)S(1)} collective-permute-done((bf16[1024,1024]{1,0:T(8,128)(2,1)S(1)}, bf16[1024,1024]{1,0:T(8,128)(2,1)S(1)}, u32[]{:S(2)}, u32[]{:S(2)}) %collective-permute-start.7) | collective-permute-done | bytes 2097184 | tf_op jit(solution)/shard_map/ppermute | solution.py:18
  512.5 2.9 constant_dynamic-update-slice_fusion.15
  521.3 15.0 %fusion.3 = f32[1280,2048]{1,0:T(8,128)S(1)} fusion(bf16[1280,2048]{1,0:T(8,128)(2,1)} %all-gather.6.cloned.1.call-done, bf16[4096,2048]{1,0:T(8,128)(2,1)} %constant_dynamic-update-slice_fusion.12, s32[]{:T(128)S(6)} %select_n.63), kind=kOutput, calls=%fused_computation.11 | convolution fusion | flops 10737418240 | bytes 24117252 | tf_op jit(solution)/shard_map/dot_general | solution.py:66
  541.8 9.6 convolution_convert_fusion.3
  551.4 86.2 %reduce-scatter.11.cloned.1.call-done = bf16[160,2048]{1,0:T(8,128)(2,1)} async-done(((bf16[1280,2048]{1,0:T(8,128)(2,1)}), bf16[160,2048]{1,0:T(8,128)(2,1)}) %reduce-scatter.11.cloned.1.call-update) | async-done | bytes 655376 | tf_op jit(solution)/shard_map/reduce_scatter | solution.py:94
  643.2 54.5 %all-gather.8.cloned.1.call-done = bf16[1280,2048]{1,0:T(8,128)(2,1)} async-done(((bf16[160,2048]{1,0:T(8,128)(2,1)}), bf16[1280,2048]{1,0:T(8,128)(2,1)}) %all-gather.8.cloned.1.call-update) | async-done | bytes 5242896 | tf_op jit(solution)/shard_map/all_gather | solution.py:90
  697.7 13.0 %multiply_convert_fusion.1 = (bf16[1280,1024]{1,0:T(8,128)(2,1)S(1)}, bf16[1280,1024]{1,0:T(8,128)(2,1)S(1)}) fusion(f32[1280,2048]{1,0:T(8,128)} %copy-done.5, bf16[1280,2048]{1,0:T(8,128)(2,1)} %all-gather.8.cloned.1.call-done, bf16[4096,1024]{1,0:T(8,128)(2,1)} %copy-done.33, s32[]{:T(128)S(6)} %select_n.63), kind=kOutput, calls=%fused_computation.22 | convolution fusion | flops 5385748480 | bytes 25165828 | tf_op jit(solution)/shard_map/dot_general | solution.py:66
  713.1 15.3 %convolution_convert_fusion.2 = bf16[1280,2048]{1,0:T(8,128)(2,1)} fusion(bf16[4096,2048]{1,0:T(8,128)(2,1)} %constant_dynamic-update-slice_fusion.12, s32[]{:T(128)S(6)} %select_n.63, bf16[1280,1024]{1,0:T(8,128)(2,1)S(1)} %get-tuple-element.38, bf16[1280,1024]{1,0:T(8,128)(2,1)S(1)} %get-tuple-element.37), kind=kOutput, calls=%fused_computation.7 | convolution fusion | flops 10750525440 | bytes 18874372 | tf_op jit(solution)/shard_map/dot_general | solution.py:70
  728.5 58.6 %reduce-scatter.13.cloned.1.call-done = bf16[160,2048]{1,0:T(8,128)(2,1)} async-done(((bf16[1280,2048]{1,0:T(8,128)(2,1)}), bf16[160,2048]{1,0:T(8,128)(2,1)}) %reduce-scatter.13.cloned.1.call-update) | async-done | bytes 655376 | tf_op jit(solution)/shard_map/reduce_scatter | solution.py:94
  788.8 3.1 fusion.52
  792.2 10.3 convolution_convert_fusion.5
  802.5 16.7 %convolution_convert_fusion = bf16[2048,2048]{1,0:T(8,128)(2,1)} fusion(bf16[1280,2048]{1,0:T(8,128)(2,1)} %all-gather.6.cloned.1.call-done, bf16[1280,1024]{1,0:T(8,128)(2,1)} %copy-done.42, bf16[1280,1024]{1,0:T(8,128)(2,1)} %copy-done.41), kind=kOutput, calls=%fused_computation.5 | convolution fusion | flops 10752098304 | bytes 18874368 | tf_op jit(solution)/shard_map/dot_general | solution.py:74
  819.6 27.1 %all-gather.10.cloned.1.call-done = bf16[1280,2048]{1,0:T(8,128)(2,1)} async-done(((bf16[160,2048]{1,0:T(8,128)(2,1)}), bf16[1280,2048]{1,0:T(8,128)(2,1)}) %all-gather.10.cloned.1.call-update) | async-done | bytes 5242896 | tf_op jit(solution)/shard_map/all_gather | solution.py:90
  846.7 4.7 multiply_reduce_fusion.2
  851.4 6.3 fusion.1
  865.4 22.7 %psum.15 = f32[2,1280]{1,0:T(2,128)S(1)} all-reduce(f32[2,1280]{1,0:T(2,128)S(1)} %pad_maximum_fusion.15), channel_id=1, replica_groups=mesh['dp'=4,'seq'=8] {'seq'}, use_global_device_ids=true, to_apply=%region_14.15 | all-reduce | flops 2560 | bytes 20480 | tf_op jit(solution)/shard_map/psum | solution.py:227
  888.1 5.4 convolution_convert_fusion.6
  894.0 2.6 multiply_convert_fusion.4
  896.7 7.5 fusion.35
  904.2 5.6 fusion.24
  913.8 8.1 convolution_convert_fusion.1
  921.9 33.5 %all_to_all.126 = bf16[8,64,1024]{2,1,0:T(8,128)(2,1)} all-to-all(bf16[8,64,1024]{2,1,0:T(8,128)(2,1)} %bitcast.207), channel_id=1, replica_groups=mesh['dp'=4,'seq'=8] {'seq'}, dimensions={0} | all-to-all | bytes 2097152 | tf_op jit(solution)/shard_map/all_to_all | solution.py:102
  955.4 36.8 %reduce-scatter.21.cloned.1.call-done = bf16[512,2048]{1,0:T(8,128)(2,1)} async-done(((bf16[2048,2048]{1,0:T(8,128)(2,1)}), bf16[512,2048]{1,0:T(8,128)(2,1)}) %reduce-scatter.21.cloned.1.call-update) | async-done | bytes 2097168 | tf_op jit(solution)/shard_map/reduce_scatter | solution.py:100
  992.3 51.5 %all_to_all.127 = bf16[8,64,2048]{2,1,0:T(8,128)(2,1)S(1)} all-to-all(bf16[8,64,2048]{2,1,0:T(8,128)(2,1)} %bitcast.199), channel_id=1, replica_groups=mesh['dp'=4,'seq'=8] {'seq'}, dimensions={0} | all-to-all | bytes 4194304 | tf_op jit(solution)/shard_map/all_to_all | solution.py:102
  1043.8 6.3 all-to-all-start.5
  1050.1 24.9 %reduce-scatter.17.cloned.1.call-done = bf16[512,896]{0,1:T(8,128)(2,1)} async-done(((bf16[2048,896]{0,1:T(8,128)(2,1)}), bf16[512,896]{0,1:T(8,128)(2,1)}) %reduce-scatter.17.cloned.1.call-update) | async-done | bytes 917520 | tf_op jit(solution)/shard_map/reduce_scatter | solution.py:100
  1077.2 5.5 all-to-all-start.4
  1089.9 26.8 %all-to-all-done.4 = bf16[8,64,896]{2,1,0:T(8,128)(2,1)} async-done(((bf16[8,64,896]{2,1,0:T(8,128)(2,1)}), bf16[8,64,896]{2,1,0:T(8,128)(2,1)}, u32[]{:S(2)}, u32[]{:S(2)}) %all-to-all-start.4) | async-done | bytes 917536 | tf_op jit(solution)/shard_map/all_to_all | solution.py:102
  1122.2 32.8 %reduce-scatter.15.cloned.1.call-done = bf16[160,2048]{1,0:T(8,128)(2,1)} async-done(((bf16[1280,2048]{1,0:T(8,128)(2,1)}), bf16[160,2048]{1,0:T(8,128)(2,1)}) %reduce-scatter.15.cloned.1.call-update) | async-done | bytes 655376 | tf_op jit(solution)/shard_map/reduce_scatter | solution.py:94
  (245 shorter events, 100.6 us)
Async XLA Ops:
  7.2 9.8 copy-start.26
  7.2 9.9 copy-start.27
  7.2 9.9 copy-start.28
  7.2 130.2 %all-gather.12.cloned.1.call-start = ((), (), s32[]{:S(2)}) async-start(), calls=%async_computation.27 | async-start | bytes 5898240 | tf_op jit(solution)/shard_map/all_gather | solution.py:90
  9.9 8.4 copy-start.40
  9.9 9.6 copy-start.38
  9.9 10.2 copy-start.39
  10.7 23.4 %all-to-all-start.1 = ((bf16[64,8,384]{2,0,1:T(8,128)(2,1)}), bf16[64,8,384]{2,0,1:T(8,128)(2,1)S(1)}, u32[]{:S(2)}, u32[]{:S(2)}) async-start(bf16[64,8,384]{2,0,1:T(8,128)(2,1)} %copy.115), calls=%async_computation.1 | async-start | bytes 786432 | tf_op jit(solution)/shard_map/all_to_all | solution.py:85
  34.1 44.9 %all-to-all-start = ((bf16[64,8,768]{2,0,1:T(8,128)(2,1)}), bf16[64,8,768]{2,0,1:T(8,128)(2,1)S(1)}, u32[]{:S(2)}, u32[]{:S(2)}) async-start(bf16[64,8,768]{2,0,1:T(8,128)(2,1)} %copy.113), calls=%async_computation | async-start | bytes 1572864 | tf_op jit(solution)/shard_map/all_to_all | solution.py:85
  40.9 263.2 %reduce-scatter.9.cloned.1.call-start = ((), (), s32[]{:S(2)}) async-start(), calls=%async_computation.16 | async-start | bytes 5898240 | tf_op jit(solution)/shard_map/reduce_scatter | solution.py:94
  43.7 37.4 %collective-permute-start.2 = (bf16[512,384]{1,0:T(8,128)(2,1)S(1)}, bf16[512,384]{1,0:T(8,128)(2,1)S(1)}, u32[]{:S(2)}, u32[]{:S(2)}) collective-permute-start(bf16[512,384]{1,0:T(8,128)(2,1)S(1)} %bitcast.185), channel_id=1, source_target_pairs={{0,24},{8,0},{16,8},{24,16},{1,25},{9,1},{17,9},{25,17},{2,26},{10... | collective-permute-start | bytes 1179656 | tf_op jit(solution)/shard_map/ppermute | solution.py:18
  79.0 18.7 %collective-permute-start = (bf16[512,768]{1,0:T(8,128)(2,1)S(1)}, bf16[512,768]{1,0:T(8,128)(2,1)S(1)}, u32[]{:S(2)}, u32[]{:S(2)}) collective-permute-start(bf16[512,768]{1,0:T(8,128)(2,1)S(1)} %bitcast.176), channel_id=1, source_target_pairs={{0,24},{8,0},{16,8},{24,16},{1,25},{9,1},{17,9},{25,17},{2,26},{10... | collective-permute-start | bytes 2359304 | tf_op jit(solution)/shard_map/ppermute | solution.py:18
  81.2 18.5 %collective-permute-start.3 = (bf16[1024,384]{1,0:T(8,128)(2,1)S(1)}, bf16[1024,384]{1,0:T(8,128)(2,1)S(1)}, u32[]{:S(2)}, u32[]{:S(2)}) collective-permute-start(bf16[1024,384]{1,0:T(8,128)(2,1)S(1)} %pad_maximum_fusion.11), channel_id=1, source_target_pairs={{0,16},{8,24},{16,0},{24,8},{1,17},{9,25},{17,1},{25,9},{2,18},{10... | collective-permute-start | bytes 2359304 | tf_op jit(solution)/shard_map/ppermute | solution.py:18
  97.8 35.2 %collective-permute-start.1 = (bf16[1024,768]{1,0:T(8,128)(2,1)S(1)}, bf16[1024,768]{1,0:T(8,128)(2,1)S(1)}, u32[]{:S(2)}, u32[]{:S(2)}) collective-permute-start(bf16[1024,768]{1,0:T(8,128)(2,1)S(1)} %pad_maximum_fusion.7), channel_id=1, source_target_pairs={{0,16},{8,24},{16,0},{24,8},{1,17},{9,25},{17,1},{25,9},{2,18},{10... | collective-permute-start | bytes 4718600 | tf_op jit(solution)/shard_map/ppermute | solution.py:18
  103.5 68.8 %copy-start.34 = (f32[256]{0:T(256)}, f32[256]{0:T(256)S(1)}, u32[]{:S(2)}) copy-start(f32[256]{0:T(256)S(1)} %get-tuple-element.79) | copy-start | bytes 3076
  103.5 68.8 %copy-start.36 = (f32[256]{0:T(256)}, f32[256]{0:T(256)S(1)}, u32[]{:S(2)}) copy-start(f32[256]{0:T(256)S(1)} %get-tuple-element.80) | copy-start | bytes 3076
  176.1 4.5 copy-start.13
  180.6 5.1 copy-start
  196.8 111.1 %all-to-all-start.2 = ((bf16[64,8,2048]{2,0,1:T(8,128)(2,1)}), bf16[64,8,2048]{2,0,1:T(8,128)(2,1)S(1)}, u32[]{:S(2)}, u32[]{:S(2)}) async-start(bf16[64,8,2048]{2,0,1:T(8,128)(2,1)} %copy.119), calls=%async_computation.3 | async-start | bytes 4194304 | tf_op jit(solution)/shard_map/all_to_all | solution.py:85
  206.4 314.8 %all-gather.6.cloned.1.call-start = ((), (), s32[]{:S(2)}) async-start(), calls=%async_computation.17 | async-start | bytes 5898240 | tf_op jit(solution)/shard_map/all_gather | solution.py:90
  307.8 329.9 %reduce-scatter.11.cloned.1.call-start = ((), (), s32[]{:S(2)}) async-start(), calls=%async_computation.18 | async-start | bytes 5898240 | tf_op jit(solution)/shard_map/reduce_scatter | solution.py:94
  307.9 67.3 %collective-permute-start.4 = (bf16[512,2048]{1,0:T(8,128)(2,1)S(1)}, bf16[512,2048]{1,0:T(8,128)(2,1)S(1)}, u32[]{:S(2)}, u32[]{:S(2)}) collective-permute-start(bf16[512,2048]{1,0:T(8,128)(2,1)S(1)} %bitcast.168), channel_id=1, source_target_pairs={{0,24},{8,0},{16,8},{24,16},{1,25},{9,1},{17,9},{25,17},{2,26},{10... | collective-permute-start | bytes 6291464 | tf_op jit(solution)/shard_map/ppermute | solution.py:18
  374.8 22.4 %collective-permute-start.6 = (bf16[512,1024]{1,0:T(8,128)(2,1)S(1)}, bf16[512,1024]{1,0:T(8,128)(2,1)S(1)}, u32[]{:S(2)}, u32[]{:S(2)}) collective-permute-start(bf16[512,1024]{1,0:T(8,128)(2,1)S(1)} %bitcast.172), channel_id=1, source_target_pairs={{0,24},{8,0},{16,8},{24,16},{1,25},{9,1},{17,9},{25,17},{2,26},{10... | collective-permute-start | bytes 3145736 | tf_op jit(solution)/shard_map/ppermute | solution.py:18
  375.7 136.8 %collective-permute-start.5 = (bf16[1024,2048]{1,0:T(8,128)(2,1)S(1)}, bf16[1024,2048]{1,0:T(8,128)(2,1)S(1)}, u32[]{:S(2)}, u32[]{:S(2)}) collective-permute-start(bf16[1024,2048]{1,0:T(8,128)(2,1)S(1)} %pad_maximum_fusion.1), channel_id=1, source_target_pairs={{0,16},{8,24},{16,0},{24,8},{1,17},{9,25},{17,1},{25,9},{2,18},{10... | collective-permute-start | bytes 12582920 | tf_op jit(solution)/shard_map/ppermute | solution.py:18
  397.4 112.8 %collective-permute-start.7 = (bf16[1024,1024]{1,0:T(8,128)(2,1)S(1)}, bf16[1024,1024]{1,0:T(8,128)(2,1)S(1)}, u32[]{:S(2)}, u32[]{:S(2)}) collective-permute-start(bf16[1024,1024]{1,0:T(8,128)(2,1)S(1)} %pad_maximum_fusion.5), channel_id=1, source_target_pairs={{0,16},{8,24},{16,0},{24,8},{1,17},{9,25},{17,1},{25,9},{2,18},{10... | collective-permute-start | bytes 6291464 | tf_op jit(solution)/shard_map/ppermute | solution.py:18
  510.7 5.2 copy-start.33
  536.3 3.9 copy-start.5
  551.4 87.6 %copy-start.3 = (bf16[1,160,2048]{2,1,0:T(8,128)(2,1)S(1)}, bf16[1,160,2048]{2,1,0:T(8,128)(2,1)}, u32[]{:S(2)}) copy-start(bf16[1,160,2048]{2,1,0:T(8,128)(2,1)} %param.28) | copy-start | bytes 1966084
  551.4 146.3 %all-gather.8.cloned.1.call-start = ((), (), s32[]{:S(2)}) async-start(), calls=%async_computation.19 | async-start | bytes 5898240 | tf_op jit(solution)/shard_map/all_gather | solution.py:90
  643.0 144.1 %reduce-scatter.13.cloned.1.call-start = ((), (), s32[]{:S(2)}) async-start(), calls=%async_computation.20 | async-start | bytes 5898240 | tf_op jit(solution)/shard_map/reduce_scatter | solution.py:94
  728.4 58.7 %copy-start.4 = (bf16[160,2048]{1,0:T(8,128)(2,1)S(1)}, bf16[160,2048]{1,0:T(8,128)(2,1)}, u32[]{:S(2)}) copy-start(bf16[160,2048]{1,0:T(8,128)(2,1)} %reduce-scatter.9.cloned.1.call-done) | copy-start | bytes 1966084
  728.4 60.4 %copy-start.6 = (bf16[160,2048]{1,0:T(8,128)(2,1)S(1)}, bf16[160,2048]{1,0:T(8,128)(2,1)}, u32[]{:S(2)}) copy-start(bf16[160,2048]{1,0:T(8,128)(2,1)} %reduce-scatter.11.cloned.1.call-done) | copy-start | bytes 1966084
  728.4 118.3 %all-gather.10.cloned.1.call-start = ((), (), s32[]{:S(2)}) async-start(), calls=%async_computation.21 | async-start | bytes 5898240 | tf_op jit(solution)/shard_map/all_gather | solution.py:90
  791.9 130.0 %reduce-scatter.23.cloned.1.call-start = ((), (), s32[]{:S(2)}) async-start(), calls=%async_computation.26 | async-start | bytes 5242880 | tf_op jit(solution)/shard_map/reduce_scatter | solution.py:100
  802.5 189.8 %reduce-scatter.21.cloned.1.call-start = ((), (), s32[]{:S(2)}) async-start(), calls=%async_computation.25 | async-start | bytes 10485760 | tf_op jit(solution)/shard_map/reduce_scatter | solution.py:100
  819.2 224.5 %reduce-scatter.19.cloned.1.call-start = ((), (), s32[]{:S(2)}) async-start(), calls=%async_computation.24 | async-start | bytes 1310720 | tf_op jit(solution)/shard_map/reduce_scatter | solution.py:100
  851.4 6.4 copy-start.9
  851.4 6.3 copy-start.14
  893.6 181.4 %reduce-scatter.17.cloned.1.call-start = ((), (), s32[]{:S(2)}) async-start(), calls=%async_computation.23 | async-start | bytes 4587520 | tf_op jit(solution)/shard_map/reduce_scatter | solution.py:100
  894.0 2.7 copy-start.10
  894.0 10.2 slice-start
  896.6 7.6 copy-start.22
  896.6 7.6 copy-start.24
  896.7 7.5 slice-start.1
  912.2 242.8 %reduce-scatter.15.cloned.1.call-start = ((), (), s32[]{:S(2)}) async-start(), calls=%async_computation.22 | async-start | bytes 5898240 | tf_op jit(solution)/shard_map/reduce_scatter | solution.py:94
  1043.8 33.4 %all-to-all-start.5 = ((bf16[8,64,256]{2,1,0:T(8,128)(2,1)}), bf16[8,64,256]{2,1,0:T(8,128)(2,1)S(1)}, u32[]{:S(2)}, u32[]{:S(2)}) async-start(bf16[8,64,256]{2,1,0:T(8,128)(2,1)} %bitcast.224), calls=%async_computation.11 | async-start | bytes 524288 | tf_op jit(solution)/shard_map/all_to_all | solution.py:102
  1077.2 39.4 %all-to-all-start.4 = ((bf16[8,64,896]{2,1,0:T(8,128)(2,1)}), bf16[8,64,896]{2,1,0:T(8,128)(2,1)}, u32[]{:S(2)}, u32[]{:S(2)}) async-start(bf16[8,64,896]{2,1,0:T(8,128)(2,1)} %bitcast.198), calls=%async_computation.9 | async-start | bytes 1835008 | tf_op jit(solution)/shard_map/all_to_all | solution.py:102
  1089.9 65.1 %copy-start.8 = (bf16[160,2048]{1,0:T(8,128)(2,1)S(1)}, bf16[160,2048]{1,0:T(8,128)(2,1)}, u32[]{:S(2)}) copy-start(bf16[160,2048]{1,0:T(8,128)(2,1)} %reduce-scatter.13.cloned.1.call-done) | copy-start | bytes 1966084
  (22 other events, 38.2 us)
Sparse Core Ops, SparseCore 0:
  9.7 75.1 all-gather.11
  191.8 112.1 reduce-scatter.8
  307.9 82.6 all-gather.5
  551.5 86.0 reduce-scatter.10
  643.1 54.5 all-gather.7
  728.5 58.4 reduce-scatter.12
  792.1 54.5 all-gather.9
  849.6 52.8 reduce-scatter.22
  905.9 86.3 reduce-scatter.20
  995.6 27.7 reduce-scatter.18
  1026.6 48.3 reduce-scatter.16
  1077.3 77.6 reduce-scatter.14
